TPU v7x, 128 devices: a whole 4x4x4 slice. The times are simulated.
128 devices in a mesh: dense: 32 (over x, z, core), attn: 4 (over y).
Axes of the slice: x: 4, y: 4, z: 4, core: 2. Of those that a mesh axis runs over, the one named last changes fastest.
Arguments:
- queries: bfloat16 [8192, 4096], P('dense', 'attn'), may hold values from -30 to 30
- keys: bfloat16 [8192, 1024], P('dense', 'attn'), may hold values from -13 to 13
- values: bfloat16 [8192, 1024], P('dense', 'attn'), may hold values from -24 to 24
- segments: int32 [8192], replicated, may hold values from 0 to 5, never falling along the last dimension, each value on 1 to 4096 neighbouring positions
- out_weight: bfloat16 [4096, 4096], P('attn', 'dense'), may hold values from -0.09375 to 0.09375
Outputs:
- projected: bfloat16 [8192, 4096], P('dense', 'attn')
All inputs are finite; a program needn't handle non-finite values.
Results may differ from a plain program's by a relative error of at most 0.012.
Values may be sent and summed in bfloat16 or wider, within the bound.
A program may use at most 128 MiB of HBM per device.

v0:
```python
import math
import jax
import jax.numpy as jnp
from jax import lax
from jax.sharding import PartitionSpec as P

HEAD_WIDTH = 128
NEGATIVE = -1e30


def attend(query_rows, positions, query_docs, keys, values, segments):
    token_count = query_rows.shape[0]
    kv_local = keys.shape[1] // HEAD_WIDTH
    head_group = query_rows.shape[1] // HEAD_WIDTH // kv_local
    blocks_count = max(token_count // 128, 1)
    block_rows = token_count // blocks_count
    inv_root = 1.0 / math.sqrt(HEAD_WIDTH)
    query_heads = query_rows.reshape(token_count, kv_local, head_group, HEAD_WIDTH)
    initial = tuple(
        (
            (
                jnp.full((kv_local, head_group, block_rows), NEGATIVE, jnp.float32),
                jnp.zeros((kv_local, head_group, block_rows), jnp.float32),
                jnp.zeros((kv_local, head_group, block_rows, HEAD_WIDTH), jnp.float32),
            )
            for which_block in range(blocks_count)
        )
    )
    key_piece = lax.all_gather(keys, "dense", axis=0, tiled=True)
    value_piece = lax.all_gather(values, "dense", axis=0, tiled=True)
    key_count = key_piece.shape[0]
    key_positions = jnp.arange(key_count, dtype=jnp.int32)
    key_heads = key_piece.reshape(key_count, kv_local, HEAD_WIDTH)
    value_heads = value_piece.reshape(key_count, kv_local, HEAD_WIDTH)
    updated = []
    for which_block in range(blocks_count):
        lower = which_block * block_rows
        upper = lower + block_rows
        visible = (query_docs[lower:upper, None] == segments[None, :]) & (
            key_positions[None, :] <= positions[lower:upper, None]
        )
        sliced = query_heads[lower:upper]

        def compute(state):
            row_max, totals, summed = state
            scores = (
                jnp.einsum("qgjd,kgd->gjqk", sliced, key_heads, preferred_element_type=jnp.float32)
                * inv_root
            )
            scores = jnp.where(visible, scores, NEGATIVE)
            new_max = jnp.maximum(row_max, jnp.max(scores, axis=-1))
            weights = jnp.where(visible, jnp.exp(scores - new_max[..., None]), 0.0)
            totals = jnp.sum(weights, axis=-1)
            summed = jnp.einsum(
                "gjqk,kgd->gjqd",
                weights.astype(jnp.bfloat16),
                value_heads,
                preferred_element_type=jnp.float32,
            )
            return (new_max, totals, summed)

        updated.append(
            lax.cond(jnp.any(visible), compute, lambda state: state, initial[which_block])
        )
    final = tuple(updated)
    outputs = []
    for state in final:
        outputs.append(state[2] / state[1][..., None])
    attended = jnp.concatenate(outputs, axis=2).astype(jnp.bfloat16)
    return attended.transpose(2, 0, 1, 3).reshape(token_count, kv_local * head_group * HEAD_WIDTH)


def project(attended, out_weight):
    partial_sums = jnp.dot(
        attended,
        lax.all_gather(out_weight, "dense", axis=1, tiled=True),
        preferred_element_type=jnp.float32,
    )
    return lax.psum_scatter(
        partial_sums.astype(jnp.bfloat16), "attn", scatter_dimension=1, tiled=True
    )


def shards(queries, keys, values, segments, out_weight):
    device_index = lax.axis_index("dense")
    token_count = queries.shape[0]
    positions = device_index * token_count + jnp.arange(token_count, dtype=jnp.int32)
    query_docs = lax.dynamic_slice_in_dim(segments, device_index * token_count, token_count)
    attended = attend(queries, positions, query_docs, keys, values, segments)
    projected = project(attended, out_weight)
    return projected


def solution(mesh):
    return jax.shard_map(
        shards,
        mesh=mesh,
        in_specs=(
            P("dense", "attn"),
            P("dense", "attn"),
            P("dense", "attn"),
            P(),
            P("attn", "dense"),
        ),
        out_specs=P("dense", "attn"),
        check_vma=False,
    )
```

profile of v0, /device:TPU:1, one launch (start us, length us, event | category | flops | bytes accessed | tf_op | source)
XLA Modules:
  0.0 251.5 jit_solution(4987157832332547177)
XLA Ops:
  6.5 0.0 all-gather.4.cloned.1.call-start
  6.5 1.7 copy.12
  8.2 0.0 all-gather.4.cloned.1.call-update
  8.2 0.0 all-gather.6.cloned.1.call-start
  8.3 1.6 copy.13
  9.9 0.0 all-gather.6.cloned.1.call-update
  9.9 0.0 all-gather.8.cloned.1.call-start
  10.0 0.7 all-gather.8.cloned.1.call-update
  10.7 0.0 reduce-scatter.2.cloned.1.call-start
  10.7 0.8 dynamic_slice.3
  11.5 4.9 %fusion.27 = (pred[]{:T(512)}, pred[]{:T(512)}, pred[128,8192]{0,1:T(8,128)(4,1)S(1)}, pred[128,8192]{0,1:T(8,128)(4,1)S(1)}) fusion(s32[128]{0:T(128)S(1)} %get-tuple-element.63, s32[8192]{0:T(1024)} %param.12, s32[128]{0:T(128)S(1)} %get-tuple-element.60, s32[128]{0:T(128)S(1)} %get-tuple-element.64, s32[128]{0:T(128)S(1)} %get-tuple-element.59), kind=kLoop, calls=%fused_computation.38 | loop fusion | flops 8388606 | bytes 2131970 | tf_op jit(solution)/shard_map/reduce_or | solution.py:63
  17.6 44.3 %all-gather.4.cloned.1.call-done = bf16[8192,256]{0,1:T(8,128)(2,1)} async-done(((bf16[256,256]{0,1:T(8,128)(2,1)}), bf16[8192,256]{0,1:T(8,128)(2,1)}) %all-gather.4.cloned.1.call-update) | async-done | bytes 4194320 | tf_op jit(solution)/shard_map/all_gather | solution.py:29
  61.9 50.4 %all-gather.6.cloned.1.call-done = bf16[8192,256]{0,1:T(8,128)(2,1)} async-done(((bf16[256,256]{0,1:T(8,128)(2,1)}), bf16[8192,256]{0,1:T(8,128)(2,1)}) %all-gather.6.cloned.1.call-update) | async-done | bytes 4194320 | tf_op jit(solution)/shard_map/all_gather | solution.py:30
  112.2 48.2 %conditional.2 = (f32[2,4,128]{2,1,0:T(4,128)S(1)}, f32[2,4,128,128]{2,3,1,0:T(8,128)S(1)}) conditional(s32[]{:T(128)} %convert_element_type.16, () %tuple.21, (pred[128,8192]{0,1:T(8,128)(4,1)S(1)}, bf16[256,1024]{1,0:T(8,128)(2,1)}, bf16[8192,2,128]{0,2,1:T(8,128)(2,1)}, bf16[8192,2,128]{0,2,1:T(8,128)(2,1)}) %tuple.54), branch_computations={%region_1.0_spmd, %region_2.5_spmd} | conditional | flops 4404018176 | bytes 114581520 | solution.py:63
  112.2 1.2 copy.14
  113.5 16.2 %fusion = (f32[2,4,128]{2,1,0:T(4,128)S(1)}, f32[2,8192,128,4]{2,1,3,0:T(8,128)}) fusion(pred[128,8192]{0,1:T(8,128)(4,1)S(1)} %get-tuple-element.25, bf16[128,2,4,128]{0,3,2,1:T(8,128)(2,1)S(1)} %bitcast.60, bf16[8192,2,128]{0,2,1:T(8,128)(2,1)} %get-tuple-element.43), kind=kOutput, calls=%fused_computation.2 | convolution fusion | flops 2172648448 | bytes 39063552 | tf_op jit(solution)/shard_map/cond/branch_1_fun/qgjd,kgd->gjqk/dot_general | solution.py:47
  129.8 15.5 %fusion.3 = f32[2,4,128,128]{2,3,1,0:T(8,128)S(1)} fusion(f32[2,8192,128,4]{2,1,3,0:T(8,128)} %get-tuple-element.54, f32[2,4,128]{2,1,0:T(4,128)S(1)} %broadcast_maximum_fusion, pred[128,8192]{0,1:T(8,128)(4,1)S(1)} %get-tuple-element.25, bf16[8192,2,128]{0,2,1:T(8,128)(2,1)} %get-tuple-element.44), kind=kOutput, calls=%fused_computation.5 | convolution fusion | flops 2189426688 | bytes 39325696 | tf_op jit(solution)/shard_map/cond | solution.py:63
  145.2 15.2 %fusion.2 = f32[2,4,128]{2,1,0:T(4,128)S(1)} fusion(f32[2,8192,128,4]{2,1,3,0:T(8,128)} %get-tuple-element.54, f32[2,4,128]{2,1,0:T(4,128)S(1)} %broadcast_maximum_fusion, pred[128,8192]{0,1:T(8,128)(4,1)S(1)} %get-tuple-element.25), kind=kLoop, calls=%fused_computation.4 | loop fusion | flops 41942016 | bytes 34611200 | tf_op jit(solution)/shard_map/cond/branch_1_fun/reduce_sum | solution.py:53
  160.4 47.9 %conditional.3 = (f32[2,4,128]{2,1,0:T(4,128)S(1)}, f32[2,4,128,128]{2,3,1,0:T(8,128)S(1)}) conditional(s32[]{:T(128)} %convert_element_type.17, () %tuple.23, (pred[128,8192]{0,1:T(8,128)(4,1)S(1)}, bf16[256,1024]{1,0:T(8,128)(2,1)}, bf16[8192,2,128]{0,2,1:T(8,128)(2,1)}, bf16[8192,2,128]{0,2,1:T(8,128)(2,1)}) %tuple.55), branch_computations={%region_6.7_spmd, %region_7.10_spmd} | conditional | flops 4404018176 | bytes 114581520 | solution.py:63
  160.6 1.2 copy.18
  161.9 16.3 %fusion.12 = (f32[2,4,128]{2,1,0:T(4,128)S(1)}, f32[2,8192,128,4]{2,1,3,0:T(8,128)}) fusion(pred[128,8192]{0,1:T(8,128)(4,1)S(1)} %get-tuple-element.29, bf16[128,2,4,128]{0,3,2,1:T(8,128)(2,1)S(1)} %bitcast.61, bf16[8192,2,128]{0,2,1:T(8,128)(2,1)} %get-tuple-element.47), kind=kOutput, calls=%fused_computation.16 | convolution fusion | flops 2172648448 | bytes 39063552 | tf_op jit(solution)/shard_map/cond/branch_1_fun/qgjd,kgd->gjqk/dot_general | solution.py:47
  178.3 15.4 %fusion.15 = f32[2,4,128,128]{2,3,1,0:T(8,128)S(1)} fusion(f32[2,8192,128,4]{2,1,3,0:T(8,128)} %get-tuple-element.56, f32[2,4,128]{2,1,0:T(4,128)S(1)} %broadcast_maximum_fusion.1, pred[128,8192]{0,1:T(8,128)(4,1)S(1)} %get-tuple-element.29, bf16[8192,2,128]{0,2,1:T(8,128)(2,1)} %get-tuple-element.48), kind=kOutput, calls=%fused_computation.19 | convolution fusion | flops 2189426688 | bytes 39325696 | tf_op jit(solution)/shard_map/cond | solution.py:63
  193.7 14.7 %fusion.14 = f32[2,4,128]{2,1,0:T(4,128)S(1)} fusion(f32[2,8192,128,4]{2,1,3,0:T(8,128)} %get-tuple-element.56, f32[2,4,128]{2,1,0:T(4,128)S(1)} %broadcast_maximum_fusion.1, pred[128,8192]{0,1:T(8,128)(4,1)S(1)} %get-tuple-element.29), kind=kLoop, calls=%fused_computation.18 | loop fusion | flops 41942016 | bytes 34611200 | tf_op jit(solution)/shard_map/cond/branch_1_fun/reduce_sum | solution.py:53
  208.3 0.1 divide_convert_fusion.1
  208.4 0.1 divide_convert_fusion
  208.5 0.1 pad_maximum_fusion
  208.5 0.0 all-gather.8.cloned.1.call-done
  208.6 7.1 %convolution_convert_fusion = bf16[256,4096]{1,0:T(8,128)(2,1)} fusion(bf16[256,1024]{0,1:T(8,128)(2,1)S(1)} %bitcast.59, bf16[1024,4096]{1,0:T(8,128)(2,1)} %all-gather.8.cloned.1.call-done), kind=kOutput, calls=%fused_computation.28 | convolution fusion | flops 2148532224 | bytes 11010048 | tf_op jit(solution)/shard_map/dot_general | solution.py:74
  215.7 0.0 reduce-scatter.2.cloned.1.call-update
  215.7 29.3 %reduce-scatter.2.cloned.1.call-done = bf16[256,1024]{1,0:T(8,128)(2,1)} async-done(((bf16[256,4096]{1,0:T(8,128)(2,1)}), bf16[256,1024]{1,0:T(8,128)(2,1)}) %reduce-scatter.2.cloned.1.call-update) | async-done | bytes 524304 | tf_op jit(solution)/shard_map/reduce_scatter | solution.py:79
  (6 shorter events, 0.1 us)
Async XLA Ops:
  6.5 55.3 %all-gather.4.cloned.1.call-start = ((), (), s32[]{:S(2)}) async-start(), calls=%async_computation.1 | async-start | bytes 4325376 | tf_op jit(solution)/shard_map/all_gather | solution.py:29
  8.2 104.0 %all-gather.6.cloned.1.call-start = ((), (), s32[]{:S(2)}) async-start(), calls=%async_computation.2 | async-start | bytes 4325376 | tf_op jit(solution)/shard_map/all_gather | solution.py:30
  9.9 198.6 %all-gather.8.cloned.1.call-start = ((), (), s32[]{:S(2)}) async-start(), calls=%async_computation.3 | async-start | bytes 8650752 | tf_op jit(solution)/shard_map/all_gather | solution.py:76
  10.7 234.3 %reduce-scatter.2.cloned.1.call-start = ((), (), s32[]{:S(2)}) async-start(), calls=%async_computation.4 | async-start | bytes 2621440 | tf_op jit(solution)/shard_map/reduce_scatter | solution.py:79
Sparse Core Ops, SparseCore 0:
  9.5 52.3 all-gather.3
  64.0 48.1 all-gather.5
  114.4 58.3 all-gather.7
  215.8 29.1 reduce-scatter.1
where the time goes:
time: 252 us
  waiting for transfers between devices  125 us (50%)
  matrix products  70.6 us (28%)
  other arithmetic  35 us (14%)
  between operations  14.3 us (6%)
  local copies, waits for them, and re-layouts  6.61 us (3%)
    all_gather x1, waiting for transfers between devices, attend(): value_piece = lax.all_gather(values, 'dense', axis=0, tiled=True)  50.4 us
    all_gather x1, waiting for transfers between devices, attend(): key_piece = lax.all_gather(keys, 'dense', axis=0, tiled=True)  44.3 us
    dot_general x2, matrix products, compute(): jnp.einsum('qgjd,kgd->gjqk', sliced, key_heads, preferred_element_type=jn...  32.6 us
    cond x2, matrix products, attend(): lax.cond(jnp.any(visible), compute, lambda state: state, initial[which_bl...  30.9 us
    reduce_sum x2, other arithmetic, compute(): totals = jnp.sum(weights, axis=-1)  29.9 us
    reduce_scatter x1, waiting for transfers between devices, project(): lax.psum_scatter(partial_sums.astype(jnp.bfloat16), 'attn', scatter_dimen...  29.3 us
    dot_general x1, matrix products, project(): jnp.dot(attended, lax.all_gather(out_weight, 'dense', axis=1, tiled=True)...  7.11 us
  transfers between devices with their start and end apart: 4, of which 3 were waited for; matrix products, arithmetic and copies ran while one was open for 41% of the time, Pallas kernels for 0%

commit v1 on v0

--- a/solution.py
+++ b/solution.py
@@ -27,7 +27,9 @@
         )
     )
     key_piece = lax.all_gather(keys, "dense", axis=0, tiled=True)
-    value_piece = lax.all_gather(values, "dense", axis=0, tiled=True)
+    value_piece = jnp.concatenate(
+        lax.all_to_all(jnp.stack([values] * lax.axis_size("dense")), "dense", 0, 0), axis=0
+    )
     key_count = key_piece.shape[0]
     key_positions = jnp.arange(key_count, dtype=jnp.int32)
     key_heads = key_piece.reshape(key_count, kv_local, HEAD_WIDTH)

time: 252 us -> 234 us (0.929)
  waiting for transfers between devices: 125 us -> 80.6 us
  local copies, waits for them, and re-layouts: 6.61 us -> 22.4 us
  starting transfers between devices: 0.12 us -> 9.56 us
    all_gather x1 -> x0, waiting for transfers between devices: 50.4 us -> none  [attend(): value_piece = lax.all_gather(values, 'dense', axis=0, tiled=True)]
    all_to_all x0 -> x1, waiting for transfers between devices: none -> 47.2 us  [attend(): lax.all_to_all(jnp.stack([values] * lax.axis_size('dense')), 'dense', 0, 0)]
    all_gather x1, waiting for transfers between devices: 44.3 us -> 1.06 us  [attend(): key_piece = lax.all_gather(keys, 'dense', axis=0, tiled=True)]
    another operation x2 -> x4, local copies, waits for them, and re-layouts: 2.49 us -> 12.4 us  [the longest x1 7.47 us: attend(): value_heads = value_piece.reshape(key_count, kv_local, HEAD_WIDTH)]
    all_to_all x0 -> x1, starting transfers between devices: none -> 9.47 us  [attend(): lax.all_to_all(jnp.stack([values] * lax.axis_size('dense')), 'dense', 0, 0)]
    all_to_all x0 -> x1, local copies, waits for them, and re-layouts: none -> 6.53 us  [attend(): lax.all_to_all(jnp.stack([values] * lax.axis_size('dense')), 'dense', 0, 0)]
  transfers between devices with their start and end apart: 4 -> 4, of which waited for: 3 -> 3; matrix products, arithmetic and copies ran while one was open for 41% -> 51% of each run, Pallas kernels for 0% -> 0%
where the time goes in v1:
time: 234 us; the launch traced here: 233 us
  waiting for transfers between devices  80.6 us (34%)
  matrix products  70.4 us (30%)
  other arithmetic  35.3 us (15%)
  local copies, waits for them, and re-layouts  22.4 us (10%)
  between operations  14.4 us (6%)
  starting transfers between devices  9.56 us (4%)
    all_to_all x1, waiting for transfers between devices, attend(): lax.all_to_all(jnp.stack([values] * lax.axis_size('dense')), 'dense', 0, 0)  47.2 us
    dot_general x2, matrix products, compute(): jnp.einsum('qgjd,kgd->gjqk', sliced, key_heads, preferred_element_type=jn...  32.4 us
    reduce_scatter x1, waiting for transfers between devices, project(): lax.psum_scatter(partial_sums.astype(jnp.bfloat16), 'attn', scatter_dimen...  31.6 us
    cond x2, matrix products, attend(): lax.cond(jnp.any(visible), compute, lambda state: state, initial[which_bl...  30.9 us
    reduce_sum x2, other arithmetic, compute(): totals = jnp.sum(weights, axis=-1)  30.1 us
    all_to_all x1, starting transfers between devices, attend(): lax.all_to_all(jnp.stack([values] * lax.axis_size('dense')), 'dense', 0, 0)  9.47 us
    another operation x1, local copies, waits for them, and re-layouts, attend(): value_heads = value_piece.reshape(key_count, kv_local, HEAD_WIDTH)  7.47 us
    dot_general x1, matrix products, project(): jnp.dot(attended, lax.all_gather(out_weight, 'dense', axis=1, tiled=True)...  7.11 us
  transfers between devices with their start and end apart: 4, of which 3 were waited for; matrix products, arithmetic and copies ran while one was open for 51% of the time, Pallas kernels for 0%

profile of v1, /device:TPU:1, one launch (start us, length us, event | category | flops | bytes accessed | tf_op | source)
XLA Modules:
  0.0 233.0 jit_solution(6694397534285832988)
XLA Ops:
  6.5 0.0 all-gather.3.cloned.1.call-start
  6.5 1.7 copy.26
  8.2 0.0 all-gather.3.cloned.1.call-update
  8.2 0.0 all-gather.5.cloned.1.call-start
  8.3 0.7 all-gather.5.cloned.1.call-update
  9.0 1.0 copy.27
  10.0 2.4 %stack.2 = bf16[32,256,256]{1,2,0:T(8,128)(2,1)} broadcast(bf16[256,256]{0,1:T(8,128)(2,1)S(1)} %copy.27), dimensions={1,2} | broadcast | bytes 4325376 | tf_op jit(solution)/shard_map/stack | solution.py:31
  12.4 9.5 %all-to-all-start = ((bf16[32,256,256]{1,2,0:T(8,128)(2,1)}), bf16[32,256,256]{1,2,0:T(8,128)(2,1)}, u32[]{:S(2)}, u32[]{:S(2)}) async-start(bf16[32,256,256]{1,2,0:T(8,128)(2,1)} %stack.2), calls=%async_computation | async-start | bytes 8388608 | tf_op jit(solution)/shard_map/all_to_all | solution.py:31
  21.9 0.0 reduce-scatter.2.cloned.1.call-start
  22.0 0.8 dynamic_slice.3
  22.7 4.9 %fusion.27 = (pred[]{:T(512)}, pred[]{:T(512)}, pred[128,8192]{0,1:T(8,128)(4,1)S(1)}, pred[128,8192]{0,1:T(8,128)(4,1)S(1)}) fusion(s32[128]{0:T(128)S(1)} %get-tuple-element.71, s32[8192]{0:T(1024)} %param.12, s32[128]{0:T(128)S(1)} %get-tuple-element.68, s32[128]{0:T(128)S(1)} %get-tuple-element.72, s32[128]{0:T(128)S(1)} %get-tuple-element.67), kind=kLoop, calls=%fused_computation.38 | loop fusion | flops 8388606 | bytes 2131970 | tf_op jit(solution)/shard_map/reduce_or | solution.py:65
  29.0 47.2 %all-to-all-done = bf16[32,256,256]{1,2,0:T(8,128)(2,1)} async-done(((bf16[32,256,256]{1,2,0:T(8,128)(2,1)}), bf16[32,256,256]{1,2,0:T(8,128)(2,1)}, u32[]{:S(2)}, u32[]{:S(2)}) %all-to-all-start) | async-done | bytes 4194336 | tf_op jit(solution)/shard_map/all_to_all | solution.py:31
  76.1 6.5 %copy.28 = bf16[32,256,256]{1,0,2:T(8,128)(2,1)} copy(bf16[32,256,256]{1,2,0:T(8,128)(2,1)} %all-to-all-done) | data formatting | bytes 8388608 | tf_op jit(solution)/shard_map/all_to_all | solution.py:31
  82.7 7.5 %reshape_reshape.3 = bf16[8192,2,128]{0,2,1:T(8,128)(2,1)} reshape(bf16[32,256,256]{1,0,2:T(8,128)(2,1)} %copy.28) | data formatting | bytes 8388608 | tf_op jit(solution)/shard_map/reshape;reshape | solution.py:36
  90.1 1.1 all-gather.3.cloned.1.call-done
  91.2 48.5 %conditional.2 = (f32[2,4,128]{2,1,0:T(4,128)S(1)}, f32[2,4,128,128]{2,3,1,0:T(8,128)S(1)}) conditional(s32[]{:T(128)} %convert_element_type.16, () %tuple.21, (pred[128,8192]{0,1:T(8,128)(4,1)S(1)}, bf16[256,1024]{1,0:T(8,128)(2,1)}, bf16[8192,2,128]{0,2,1:T(8,128)(2,1)}, bf16[8192,2,128]{0,2,1:T(8,128)(2,1)}) %tuple.52), branch_computations={%region_1.0_spmd, %region_2.5_spmd} | conditional | flops 4404018176 | bytes 114581520 | solution.py:65
  91.2 1.2 copy.29
  92.5 16.2 %fusion = (f32[2,4,128]{2,1,0:T(4,128)S(1)}, f32[2,8192,128,4]{2,1,3,0:T(8,128)}) fusion(pred[128,8192]{0,1:T(8,128)(4,1)S(1)} %get-tuple-element.25, bf16[128,2,4,128]{0,3,2,1:T(8,128)(2,1)S(1)} %bitcast.61, bf16[8192,2,128]{0,2,1:T(8,128)(2,1)} %get-tuple-element.51), kind=kOutput, calls=%fused_computation.2 | convolution fusion | flops 2172648448 | bytes 39063552 | tf_op jit(solution)/shard_map/cond/branch_1_fun/qgjd,kgd->gjqk/dot_general | solution.py:49
  108.7 15.5 %fusion.3 = f32[2,4,128,128]{2,3,1,0:T(8,128)S(1)} fusion(f32[2,8192,128,4]{2,1,3,0:T(8,128)} %get-tuple-element.62, f32[2,4,128]{2,1,0:T(4,128)S(1)} %broadcast_maximum_fusion, pred[128,8192]{0,1:T(8,128)(4,1)S(1)} %get-tuple-element.25, bf16[8192,2,128]{0,2,1:T(8,128)(2,1)} %get-tuple-element.52), kind=kOutput, calls=%fused_computation.5 | convolution fusion | flops 2189426688 | bytes 39325696 | tf_op jit(solution)/shard_map/cond | solution.py:65
  124.2 15.4 %fusion.2 = f32[2,4,128]{2,1,0:T(4,128)S(1)} fusion(f32[2,8192,128,4]{2,1,3,0:T(8,128)} %get-tuple-element.62, f32[2,4,128]{2,1,0:T(4,128)S(1)} %broadcast_maximum_fusion, pred[128,8192]{0,1:T(8,128)(4,1)S(1)} %get-tuple-element.25), kind=kLoop, calls=%fused_computation.4 | loop fusion | flops 41942016 | bytes 34611200 | tf_op jit(solution)/shard_map/cond/branch_1_fun/reduce_sum | solution.py:55
  139.6 47.8 %conditional.3 = (f32[2,4,128]{2,1,0:T(4,128)S(1)}, f32[2,4,128,128]{2,3,1,0:T(8,128)S(1)}) conditional(s32[]{:T(128)} %convert_element_type.17, () %tuple.23, (pred[128,8192]{0,1:T(8,128)(4,1)S(1)}, bf16[256,1024]{1,0:T(8,128)(2,1)}, bf16[8192,2,128]{0,2,1:T(8,128)(2,1)}, bf16[8192,2,128]{0,2,1:T(8,128)(2,1)}) %tuple.53), branch_computations={%region_6.7_spmd, %region_7.10_spmd} | conditional | flops 4404018176 | bytes 114581520 | solution.py:65
  139.9 1.2 copy.33
  141.2 16.2 %fusion.12 = (f32[2,4,128]{2,1,0:T(4,128)S(1)}, f32[2,8192,128,4]{2,1,3,0:T(8,128)}) fusion(pred[128,8192]{0,1:T(8,128)(4,1)S(1)} %get-tuple-element.29, bf16[128,2,4,128]{0,3,2,1:T(8,128)(2,1)S(1)} %bitcast.62, bf16[8192,2,128]{0,2,1:T(8,128)(2,1)} %get-tuple-element.55), kind=kOutput, calls=%fused_computation.16 | convolution fusion | flops 2172648448 | bytes 39063552 | tf_op jit(solution)/shard_map/cond/branch_1_fun/qgjd,kgd->gjqk/dot_general | solution.py:49
  157.4 15.4 %fusion.15 = f32[2,4,128,128]{2,3,1,0:T(8,128)S(1)} fusion(f32[2,8192,128,4]{2,1,3,0:T(8,128)} %get-tuple-element.64, f32[2,4,128]{2,1,0:T(4,128)S(1)} %broadcast_maximum_fusion.1, pred[128,8192]{0,1:T(8,128)(4,1)S(1)} %get-tuple-element.29, bf16[8192,2,128]{0,2,1:T(8,128)(2,1)} %get-tuple-element.56), kind=kOutput, calls=%fused_computation.19 | convolution fusion | flops 2189426688 | bytes 39325696 | tf_op jit(solution)/shard_map/cond | solution.py:65
  172.8 14.7 %fusion.14 = f32[2,4,128]{2,1,0:T(4,128)S(1)} fusion(f32[2,8192,128,4]{2,1,3,0:T(8,128)} %get-tuple-element.64, f32[2,4,128]{2,1,0:T(4,128)S(1)} %broadcast_maximum_fusion.1, pred[128,8192]{0,1:T(8,128)(4,1)S(1)} %get-tuple-element.29), kind=kLoop, calls=%fused_computation.18 | loop fusion | flops 41942016 | bytes 34611200 | tf_op jit(solution)/shard_map/cond/branch_1_fun/reduce_sum | solution.py:55
  187.5 0.1 divide_convert_fusion.1
  187.5 0.1 divide_convert_fusion
  187.6 0.1 pad_maximum_fusion
  187.7 0.0 all-gather.5.cloned.1.call-done
  187.7 7.1 %convolution_convert_fusion = bf16[256,4096]{1,0:T(8,128)(2,1)} fusion(bf16[256,1024]{0,1:T(8,128)(2,1)S(1)} %bitcast.60, bf16[1024,4096]{1,0:T(8,128)(2,1)} %all-gather.5.cloned.1.call-done), kind=kOutput, calls=%fused_computation.28 | convolution fusion | flops 2148532224 | bytes 11010048 | tf_op jit(solution)/shard_map/dot_general | solution.py:76
  194.8 0.0 reduce-scatter.2.cloned.1.call-update
  194.8 31.6 %reduce-scatter.2.cloned.1.call-done = bf16[256,1024]{1,0:T(8,128)(2,1)} async-done(((bf16[256,4096]{1,0:T(8,128)(2,1)}), bf16[256,1024]{1,0:T(8,128)(2,1)}) %reduce-scatter.2.cloned.1.call-update) | async-done | bytes 524304 | tf_op jit(solution)/shard_map/reduce_scatter | solution.py:81
  (6 shorter events, 0.1 us)
Async XLA Ops:
  6.5 84.6 %all-gather.3.cloned.1.call-start = ((), (), s32[]{:S(2)}) async-start(), calls=%async_computation.2 | async-start | bytes 4325376 | tf_op jit(solution)/shard_map/all_gather | solution.py:29
  8.2 179.5 %all-gather.5.cloned.1.call-start = ((), (), s32[]{:S(2)}) async-start(), calls=%async_computation.3 | async-start | bytes 8650752 | tf_op jit(solution)/shard_map/all_gather | solution.py:78
  12.4 63.7 %all-to-all-start = ((bf16[32,256,256]{1,2,0:T(8,128)(2,1)}), bf16[32,256,256]{1,2,0:T(8,128)(2,1)}, u32[]{:S(2)}, u32[]{:S(2)}) async-start(bf16[32,256,256]{1,2,0:T(8,128)(2,1)} %stack.2), calls=%async_computation | async-start | bytes 8388608 | tf_op jit(solution)/shard_map/all_to_all | solution.py:31
  21.9 204.5 %reduce-scatter.2.cloned.1.call-start = ((), (), s32[]{:S(2)}) async-start(), calls=%async_computation.4 | async-start | bytes 2621440 | tf_op jit(solution)/shard_map/reduce_scatter | solution.py:81
Sparse Core Ops, SparseCore 0:
  9.5 81.6 all-gather.2
  93.4 58.9 all-gather.4
  194.9 31.4 reduce-scatter.1
